TPU v7x, 256 devices: a whole 4x4x8 slice. The times are simulated.
256 devices in a mesh: gy: 16 (over y_hi, x, core), gx: 16 (over y_lo, z).
Axes of the slice: x: 4, y: 4 (y_hi: 2, y_lo: 2; y = y_hi * 2 + y_lo), z: 8, core: 2. Of those that a mesh axis runs over, the one named last changes fastest.
Arguments:
- stored_tiles: float32 [16, 128, 12288], P('gy', 'gx'), may hold values from -6 to 6
- tile_target: int32 [16, 128], P('gy', 'gx'), may hold values from 0 to 127, as said below
- tile_mask: int32 [16, 128], P('gy', 'gx'), may hold values 0 or 1
- stem_weight: float32 [48, 96], replicated, may hold values from -0.875 to 0.875
- stem_bias: float32 [96], replicated, may hold values from -3 to 3
- depth_weight: float32 [49, 96], replicated, may hold values from -0.875 to 0.875
- depth_bias: float32 [96], replicated, may hold values from -4 to 4
- norm_gain: float32 [96], replicated, may hold values from 0.5 to 1.5
- norm_bias: float32 [96], replicated, may hold values from -3 to 3
- expand_weight: float32 [96, 384], replicated, may hold values from -0.625 to 0.625
- expand_bias: float32 [384], replicated, may hold values from -3 to 3
- shrink_weight: float32 [384, 96], replicated, may hold values from -0.3125 to 0.3125
- shrink_bias: float32 [96], replicated, may hold values from -3 to 3
- cotangent: float32 [96, 256, 2048], P(None, 'gy', 'gx'), may hold values from -6 to 6
Outputs:
- block_out: float32 [96, 256, 2048], P(None, 'gy', 'gx')
- grad_stem_weight: float32 [48, 96], replicated
- grad_stem_bias: float32 [96], replicated
- grad_depth_weight: float32 [49, 96], replicated
- grad_depth_bias: float32 [96], replicated
- grad_norm_gain: float32 [96], replicated
- grad_norm_bias: float32 [96], replicated
- grad_expand_weight: float32 [96, 384], replicated
- grad_expand_bias: float32 [384], replicated
- grad_shrink_weight: float32 [384, 96], replicated
- grad_shrink_bias: float32 [96], replicated
Inputs may be any that keep to these rules, and one draw needn't show every extreme that they name: `tile_target`: in each row r the 128 slots hold each target 0 to 127 once; the target's grid cell is row r, column target // 8. The 8 slots of the device in column i of gx send exactly 4 tiles to each cell of column (i + 1 + k * 8) mod 16, k < 2, and none to the others.
All inputs are finite; a program needn't handle non-finite values. No bound on the sum of `tile_mask` on one device may be relied on, other than what follows from the above.
Results may differ from a plain program's by a relative error of at most 0.0003.
Values sent between devices are 32-bit elements; how exact they have to be, the bound alone decides.
A program may use at most 128 MiB of HBM per device.

v0:
```python
import jax
import jax.numpy as jnp
from jax import lax
from jax.experimental import pallas as pl
from jax.experimental.pallas import tpu as pltpu
from jax.sharding import PartitionSpec as P

C = 96
HID = 384
NB = C // 8
H = 16
W = 128
EXT = H + 6
KK = 48
TAPS = 49
PIX = 12288
f32 = jnp.float32
bf16 = jnp.bfloat16
EPS = 1e-6
MESH = pl.DeviceIdType.MESH
DMA = pltpu.SemaphoreType.DMA

NN = (((1,), (0,)), ((), ()))
NT = (((1,), (1,)), ((), ()))


def split(x):
    hi = x.astype(bf16)
    return hi, (x - hi.astype(f32)).astype(bf16)


def dot(a, b, dims=NN):
    return lax.dot_general(a, b, dims, preferred_element_type=f32)


def lanes(shape=(8, W)):
    return lax.broadcasted_iota(jnp.int32, shape, len(shape) - 1)


def roll(x, by):
    by = by % W
    return x if by == 0 else pltpu.roll(x, by, x.ndim - 1)


STEM_B, DEPTH_B, GAIN, NBIAS, SHRINK_B = 49, 50, 51, 52, 53
GROUPS = ((0, 1, 2, 13, 14, 15), (3, 4, 5, 6, 7), (8, 9, 10, 11, 12))
ORDER = tuple(h for group in GROUPS for h in group)
INFO = 2
NEAR = ((0, -1), (0, 1), (-1, -1), (-1, 1), (1, -1), (1, 1))


def payload_range(group):
    before = sum(len(g) for g in GROUPS[:group])
    after = before + len(GROUPS[group])
    return (0 if group == 0 else INFO + 3 * before), INFO + 3 * after


def row_ranges(group):
    rows = GROUPS[group]
    if group == 0:
        return ((rows[0], 3), (rows[3], 3))
    return ((rows[0], len(rows)),)


def take(x, index, axis):
    return jnp.take_along_axis(x, index, axis=axis)


def each(low, high, f):
    def one(i, _):
        f(i)
        return 0
    lax.fori_loop(low, high, one, 0)


XR = C + 16
CH = 16
SLOTS = 96
TAIL = 16
SHIFTS = (0, 1, 2, 4, 5, 6)
STEPS = (3,)

def validity(gy, gx):
    ny = lax.axis_size("gy")
    nx = lax.axis_size("gx")
    lane = lanes()
    pos = lane & 7
    prow = lane >> 3
    top_ok = (gy > 0).astype(f32)
    bot_ok = (gy < ny - 1).astype(f32)
    left_ok = (gx > 0).astype(f32)
    right_ok = (gx < nx - 1).astype(f32)
    col_ok = jnp.where(pos < 3, left_ok, jnp.where(pos < 6, right_ok, 0.0))
    col_ok = jnp.where(prow < 11, col_ok, 0.0)
    ok0 = col_ok * jnp.where(prow < 3, top_ok, 1.0)
    ok1 = col_ok * jnp.where(prow >= 8, bot_ok, 1.0)
    return top_ok, bot_ok, ok0, ok1


def whole_kernel(
    tiles_hbm, target_hbm, marks_hbm, stem_hbm, dw_hbm, sb_hbm, db_hbm, ga_hbm, nb_hbm, ew_hbm, eb_hbm, sw_hbm, hb_hbm, cot_hbm,
    out_hbm, sum_ref, tail_ref,
    pat_ref, side_ref, fm_ref, wb_ref, wbs_ref, pb_ref, stem3_ref, up2_ref, dnn2_ref, dn3_ref, upn3_ref, tiles,
    target, marks, stem_v, dw_v, sb_v, db_v, ga_v, nb_v, ew_v, eb_v, sw_v, hb_v, send, recv, edge, edges,
    edges_mid, ct, cot_ref, in_sem, par_sem, tile_send, tile_recv, row_send, row_recv, edge_send, edge_recv,
    mid_send, mid_recv, cot_sem, out_sem, F, FS, D, DSH, DY, GE, GS, ACC, FHL, FSH, SH, OUT, G, R0, B0, R1, B1,
    R2, TG, TR, TP, TX, DF, DFS, GV, s0, r0, s1, r1, s2, r2, s3, r3, s4, r4, ts1, tr1, ts2, tr2, ts3, tr3, *bufs,
):
    gy = lax.axis_index("gy")
    gx = lax.axis_index("gx")
    ny = lax.axis_size("gy")
    nx = lax.axis_size("gx")

    def device(dy, dx):
        return (lax.rem(gy + dy + ny, ny), lax.rem(gx + dx + nx, nx))

    y_hi, xx, core = gy >> 3, (gy >> 1) & 3, gy & 1
    y_lo, z = gx >> 3, gx & 7
    plane = (y_hi * 2 + y_lo) * 4 + xx

    def at_plane(m, c):
        return ((m >> 3) * 8 + (m & 3) * 2 + c, ((m >> 2) & 1) * 8 + z)

    def at_z(j):
        return (gy, y_lo * 8 + j)

    barrier = pltpu.get_barrier_semaphore()

    def greet(to):
        pl.semaphore_signal(barrier, inc=1, device_id=to, device_id_type=MESH)

    peers = [(0, 1), (0, -1), (0, 9), (0, -9)] + [(dy, dx) for dy in (-1, 1) for dx in (-1, 0, 1)]
    for dy, dx in peers:
        greet(device(dy, dx))
    each(1, 16, lambda i: greet(at_plane((plane + i) & 15, core)))
    each(0, 16, lambda i: greet(at_plane((plane + i) & 15, 1 - core)))
    each(1, 8, lambda i: greet(at_z((z + i) & 7)))
    greetings = len(peers) + 15 + 16 + 7

    params = [
        pltpu.make_async_copy(src, dst, par_sem.at[i])
        for i, (src, dst) in enumerate((
            (target_hbm, target), (marks_hbm, marks), (stem_hbm, stem_v), (dw_hbm, dw_v), (sb_hbm, sb_v),
            (db_hbm, db_v), (ga_hbm, ga_v), (nb_hbm, nb_v), (ew_hbm, ew_v), (eb_hbm, eb_v), (sw_hbm, sw_v),
            (hb_hbm, hb_v)))
    ]
    params[0].start()
    params[1].start()
    loads = []
    for group in range(len(GROUPS)):
        for lo, n in row_ranges(group):
            for k in range(3):
                at = pl.ds(k * 4096 + lo * 256, n * 256)
                loads.append((group, pltpu.make_async_copy(
                    tiles_hbm.at[:, at], tiles.at[:, at], in_sem.at[len(loads)])))
                loads[-1][1].start()
    for copy in params[2:]:
        copy.start()
    cot_copy = pltpu.make_async_copy(cot_hbm, cot_ref, cot_sem)
    cot_copy.start()

    sub = lax.broadcasted_iota(jnp.int32, (8, W), 0)
    lane = lanes()
    row8 = lax.broadcasted_iota(jnp.int32, (8, 8), 0)
    col8 = lax.broadcasted_iota(jnp.int32, (8, 8), 1)
    eye = row8 == col8
    params[0].wait()
    params[1].wait()

    def down_column(row):
        return jnp.sum(jnp.where(eye, row, 0.0), axis=1, keepdims=True)

    codes = jnp.broadcast_to(target[...], (8, 8))
    bucket = ((((codes >> 3) - gx - 1) & 15) >> 3).astype(f32)
    place = (codes & 7).astype(f32)
    mark = jnp.broadcast_to(marks[...], (8, 8)).astype(f32)
    bucket_col = down_column(bucket)
    rank = jnp.sum(jnp.where((bucket_col == bucket) & (row8 < col8), 1.0, 0.0), axis=0, keepdims=True)
    slot_pos = bucket[0:1, :] * 4.0 + rank

    def sources(wanted):
        return jnp.sum(jnp.where(slot_pos == wanted.astype(f32), col8.astype(f32), 0.0), axis=1, keepdims=True)

    order = jnp.broadcast_to(sources(row8), (8, W)).astype(jnp.int32)
    turned = jnp.broadcast_to(sources((row8 + 4) & 7), (8, W)).astype(jnp.int32)
    place_col = jnp.broadcast_to(down_column(place), (8, W))
    mark_col = jnp.broadcast_to(down_column(mark), (8, W))
    low = sub < 4

    def put(q, x0, x1):
        g0 = take(x0, order, 0)
        g1 = take(x1, turned, 0)
        send[0, q] = jnp.where(low, g0, g1)
        send[1, q] = jnp.where(low, g1, g0)

    def tile_copy(bucket_at, group):
        lo, hi = payload_range(group)
        return pltpu.make_async_remote_copy(
            src_ref=send.at[bucket_at, pl.ds(lo, hi - lo)],
            dst_ref=recv.at[bucket_at, pl.ds(lo, hi - lo)],
            send_sem=tile_send.at[bucket_at, group],
            recv_sem=tile_recv.at[bucket_at, group],
            device_id=device(0, 1 + 8 * bucket_at),
            device_id_type=MESH,
        )

    pos = lane & 7
    left = pos < 3

    def prepare():
        src = lax.broadcasted_iota(jnp.int32, (2 * W, W), 0) & (W - 1)
        dst = lax.broadcasted_iota(jnp.int32, (2 * W, W), 1)
        for n, b in enumerate(SHIFTS):
            SH[:, n * W : (n + 1) * W] = jnp.where(src == dst + (b - 3), 1.0, 0.0).astype(bf16)

        for copy in params[2:]:
            copy.wait()
        ct[...] = jnp.zeros_like(ct)
        ct[0:TAPS, 0:C] = dw_v[...]
        for k, ref in enumerate((sb_v, db_v, ga_v, nb_v, hb_v)):
            ct[STEM_B + k : STEM_B + k + 1, 0:C] = ref[...]
        cols = ct[...].T
        ct[...] = cols

        def spread(cb, _):
            cs = pl.ds(pl.multiple_of(cb * 8, 8), 8)
            wc = ct[cs, :]
            for a in range(7):
                taps = []
                for b in range(7):
                    t = 7 * a + b
                    taps.append(jnp.broadcast_to(wc[:, t : t + 1], (8, W)))
                    wb_ref[cb, t] = taps[-1]
                for k in range(3):
                    wbs_ref[cb, 3 * a + k] = jnp.where(left, taps[k], taps[6 - k])
            for k in range(5):
                pb_ref[k, cs, :] = jnp.broadcast_to(wc[:, STEM_B + k : STEM_B + k + 1], (8, W))
            return 0

        lax.fori_loop(0, NB, spread, 0)

        def turned_over(x):
            n = x.shape[0]
            return jnp.concatenate([x, jnp.zeros((W - n, x.shape[1]), f32)], axis=0).T

        stem_pad = jnp.concatenate([stem_v[...], jnp.zeros((KK, W - C), f32)], axis=1)
        hi, lo = split(turned_over(stem_pad)[:C, :KK])
        stem3_ref[:, 0:KK] = hi
        stem3_ref[:, KK : 2 * KK] = hi
        stem3_ref[:, 2 * KK :] = lo
        ew = ew_v[...]
        sw = sw_v[...]
        for src, ref in ((sw, dn3_ref), (ew, upn3_ref)):
            hi, lo = split(src)
            ref[:, 0:HID] = hi
            ref[:, HID : 2 * HID] = hi
            ref[:, 2 * HID :] = lo
        hi, lo = split(turned_over(sw)[:, :C])
        dnn2_ref[0:HID, 0:C] = hi
        dnn2_ref[0:HID, C : 2 * C] = hi
        dnn2_ref[HID:, 0:C] = lo
        dnn2_ref[HID:, C : 2 * C] = jnp.zeros((HID, C), bf16)
        up = jnp.concatenate([ew, eb_v[...], jnp.zeros((W - C - 1, HID), f32)], axis=0).T
        hi, lo = split(up[:, : C + 16])
        up2_ref[0:HID, 0 : C + 16] = hi
        up2_ref[0:HID, C + 16 :] = hi
        up2_ref[HID:, 0 : C + 16] = lo
        up2_ref[HID:, C + 16 :] = jnp.zeros((HID, C + 16), bf16)


    put(0, place_col, place_col)
    put(1, mark_col, mark_col)
    for group, rows in enumerate(GROUPS):
        for at, copy in loads:
            if at == group:
                copy.wait()
        for h in rows:
            for k in range(3):
                r = k * 32 + h * 2
                x0 = tiles[:, r * W : (r + 1) * W] * mark_col
                x1 = tiles[:, (r + 1) * W : (r + 2) * W] * mark_col
                put(INFO + 3 * ORDER.index(h) + k, x0, x1)
        if group > 0:
            for bucket_at in range(2):
                tile_copy(bucket_at, group).start()
            continue
        prepare()
        pl.semaphore_wait(barrier, greetings)
        for bucket_at in range(2):
            tile_copy(bucket_at, group).start()

    w16 = lane & 15
    beta = lane >> 4
    prow = lane >> 3

    def row_copy(up):
        src, dst, dy = (3, H + 3, -1) if up else (H, 0, 1)
        return pltpu.make_async_remote_copy(
            src_ref=pat_ref.at[pl.ds(src, 3)],
            dst_ref=pat_ref.at[pl.ds(dst, 3)],
            send_sem=row_send.at[int(up)],
            recv_sem=row_recv.at[int(up)],
            device_id=device(dy, 0),
            device_id_type=MESH,
        )

    def edge_copy(i):
        dy, dx = NEAR[i]
        return pltpu.make_async_remote_copy(
            src_ref=edge.at[0], dst_ref=edges.at[i], send_sem=edge_send.at[i], recv_sem=edge_recv.at[i],
            device_id=device(dy, dx), device_id_type=MESH)

    def mid_copy(group, i):
        dy, dx = NEAR[i]
        return pltpu.make_async_remote_copy(
            src_ref=edge.at[group], dst_ref=edges_mid.at[group - 1, i],
            send_sem=mid_send.at[group - 1, i], recv_sem=mid_recv.at[group - 1, i],
            device_id=device(dy, dx), device_id_type=MESH)

    for group, rows in enumerate(GROUPS):
        for bucket_at in range(2):
            tile_copy(bucket_at, group).wait_recv()
        if group == 0:
            places = (recv[0, 0], recv[1, 0])
            marks_in = (recv[0, 1], recv[1, 1])
            first = []
            for p in places:
                g = (beta - p.astype(jnp.int32)) & 7
                first.append((g >> 2) * 64 + w16 * 4 + (g & 3))
            wanted = ((beta - sub) & 7).astype(f32)
            wanted_t = beta.astype(f32)
            found = []
            fm = jnp.zeros((8, W), f32)
            for j, off in ((0, 0), (1, 4)):
                at = jnp.zeros((8, W), f32)
                hit = jnp.zeros((8, W), f32)
                for k in range(4):
                    p = jnp.broadcast_to(places[j][off + k : off + k + 1, :], (8, W))
                    m = jnp.broadcast_to(marks_in[j][off + k : off + k + 1, :], (8, W))
                    at = jnp.where(p == wanted, float(k), at)
                    hit = jnp.where(p == wanted, 1.0, hit)
                    fm = jnp.where(p == wanted_t, m, fm)
                found.append((at.astype(jnp.int32), hit))
            fm_ref[...] = fm
            in_a = found[0][1] > 0.0
            second = [(found[0][0] + 4 * a, found[1][0] + 4 * (1 - a)) for a in range(2)]
            third = ((sub + beta) & 7) * 16 + w16
        for h in rows:
            for k in range(3):
                q = INFO + 3 * ORDER.index(h) + k
                ya = take(recv[0, q], first[0], 1)
                yb = take(recv[1, q], first[1], 1)
                for a in range(2):
                    v = jnp.where(in_a, take(ya, second[a][0], 0), take(yb, second[a][1], 0))
                    pat_ref[h + 3, pl.ds(16 * k + 8 * a, 8), :] = take(v, third, 1)
        if group == 0:
            row_copy(True).start()
            row_copy(False).start()
        for j in range(KK // 8):
            js = pl.ds(8 * j, 8)
            v = jnp.zeros((8, W), f32)
            for h in rows:
                v = jnp.where(prow == h, roll(pat_ref[h + 3, js, :], 8 * h + 3), v)
            edge[group, js, :] = v
        if group == 0:
            for i in range(len(NEAR)):
                edge_copy(i).start()
        else:
            for i in range(2):
                mid_copy(group, i).start()

    for i in range(len(NEAR)):
        edge_copy(i).wait_recv()
    for group in (1, 2):
        for i in range(2):
            mid_copy(group, i).wait_recv()
    up_left, up_right = edges.at[5], edges.at[4]
    down_left, down_right = edges.at[3], edges.at[2]
    for j in range(KK // 8):
        js = pl.ds(8 * j, 8)
        from_left = edges[1, js, :] + (edges_mid[0, 1, js, :] + edges_mid[1, 1, js, :])
        from_right = edges[0, js, :] + (edges_mid[0, 0, js, :] + edges_mid[1, 0, js, :])
        mid = jnp.where(left, from_left, from_right)
        top = jnp.where(left, up_left[js, :], up_right[js, :])
        bottom = jnp.where(left, down_left[js, :], down_right[js, :])
        side_ref[0, js, :] = jnp.where(prow < 3, roll(top, -104), roll(mid, 24))
        side_ref[1, js, :] = jnp.where(prow < 8, roll(mid, -64), roll(bottom, 64))
    row_copy(True).wait_recv()
    row_copy(False).wait_recv()
    top_ok, bot_ok, ok0, ok1 = validity(gy, gx)
    def stem_of(p, bias):
        hi, lo = split(p)
        return dot(stem3_ref[...], jnp.concatenate([hi, lo, hi], axis=0)) + bias

    bias2 = jnp.concatenate([pb_ref[0], pb_ref[0]], axis=1)

    def row_ok(r):
        return top_ok if r < 3 else bot_ok if r >= H + 3 else None

    for r in range(0, EXT, 2):
        parts = []
        for q in range(2):
            ok = row_ok(r + q)
            p = pat_ref[r + q]
            parts.append(p if ok is None else jnp.where(ok > 0.0, p, 0.0))
        y = stem_of(jnp.concatenate(parts, axis=1), bias2)
        for q in range(2):
            ok = row_ok(r + q)
            v = y[:, q * W : (q + 1) * W]
            if ok is not None:
                v = v * ok
            F[r + q] = v
            hi, lo = split(v)
            FHL[(r + q) * C : (r + q + 1) * C, 0:W] = hi
            FHL[(r + q) * C : (r + q + 1) * C, W:] = lo
    parts = []
    for i, ok in enumerate((ok0, ok1)):
        okk = jnp.concatenate([ok] * (KK // 8), axis=0)
        parts.append(jnp.where(okk > 0.0, side_ref[i], 0.0))
    y = stem_of(jnp.concatenate(parts, axis=1), bias2)
    for i, ok in enumerate((ok0, ok1)):
        FS[i] = y[:, i * W : (i + 1) * W] * jnp.concatenate([ok] * NB, axis=0)

    def shift_rows(rows, count, put):
        for n in range(3):
            def some(i, _, n=n):
                rs = pl.ds(pl.multiple_of(i * rows, rows), rows)
                y = dot(FHL[rs, :], SH[:, 2 * n * W : (2 * n + 2) * W])
                put(2 * n, rs, y[:, :W])
                put(2 * n + 1, rs, y[:, W:])
                return 0
            lax.fori_loop(0, count, some, 0)

    def put_features(n, rs, y):
        FSH[n, rs, :] = y

    shift_rows(4 * C, 5, put_features)
    for n in range(3):
        rs = slice(20 * C, 22 * C)
        y = dot(FHL[rs, :], SH[:, 2 * n * W : (2 * n + 2) * W])
        FSH[2 * n, rs, :] = y[:, :W]
        FSH[2 * n + 1, rs, :] = y[:, W:]

    edge_lane = (lane < 3) | (lane >= W - 3)

    def conv_block(cb, _):
        cs = pl.ds(pl.multiple_of(cb * 8, 8), 8)
        part = [None] * 3
        fs0 = FS[0, cs, :]
        fs1 = FS[1, cs, :]
        for a in range(7):
            win = jnp.where(prow < 11 - a, roll(fs0, -8 * a), roll(fs1, 8 * (11 - a)))
            for k in range(3):
                t = wbs_ref[cb, 3 * a + k] * win
                part[k] = t if part[k] is None else part[k] + t
        q = part[0]
        for k in (1, 2):
            q = q + jnp.where(left, jnp.where(pos < 3 - k, roll(part[k], -k), 0.0),
                              jnp.where((pos >= 3 + k) & (pos < 6), roll(part[k], k), 0.0))
        q = jnp.where(left, roll(q, -3), roll(q, 3))
        bias = pb_ref[1, cs, :]
        acc = [bias + jnp.where(edge_lane, roll(q, 125 - 8 * h), 0.0) for h in range(H)]
        for b in range(7):
            if b == 3:
                rows = [F[r, cs, :] for r in range(EXT)]
            else:
                rows = [FSH[SHIFTS.index(b), pl.ds(pl.multiple_of(r * C + cb * 8, 8), 8), :] for r in range(EXT)]
            for a in range(7):
                w = wb_ref[cb, 7 * a + b]
                for h in range(H):
                    acc[h] = acc[h] + w * rows[h + a]
        for h in range(H):
            D[h, cs, :] = acc[h]
        return 0

    lax.fori_loop(0, NB, conv_block, 0)

    fmc = jnp.concatenate([fm_ref[...]] * NB, axis=0)
    ones_row = jnp.where(lax.broadcasted_iota(jnp.int32, (16, 2 * W), 0) == 0, 1.0, 0.0)
    lanesets = [bufs[: len(bufs) // 2], bufs[len(bufs) // 2 :]]
    for XHL, *_ in lanesets:
        XHL[C:XR, :] = ones_row.astype(bf16)
        XHL[XR + C :, :] = jnp.zeros((16, 2 * W), bf16)
    GE[...] = jnp.zeros_like(GE)
    GS[...] = jnp.zeros_like(GS)
    ACC[...] = jnp.zeros_like(ACC)

    def stage_a(i, buf):
        XHL, YHL, U, DA, AHL, GHL, XN, RS = buf
        for q in range(2):
            h = 2 * i + q
            qs = slice(q * W, (q + 1) * W)
            x = D[h]
            m = jnp.mean(x, axis=0, keepdims=True)
            xc = x - m
            v = jnp.mean(xc * xc, axis=0, keepdims=True)
            rs = lax.rsqrt(v + EPS)
            xn = xc * rs
            XN[q] = xn
            RS[q] = jnp.broadcast_to(rs, (8, W))
            hi, lo = split(xn * pb_ref[2] + pb_ref[3])
            XHL[0:C, qs] = hi
            XHL[XR : XR + C, qs] = lo
            dy = cot_ref[pl.ds(h, C, stride=H), :] * fmc
            DY[h] = dy
            ACC[3] += dy
            hi, lo = split(dy)
            YHL[0:C, qs] = hi
            YHL[C:, qs] = lo
        t = dot(up2_ref[...], XHL[...])
        U[...] = t[:HID] + t[HID:]
        t = dot(dnn2_ref[...], YHL[...])
        DA[...] = t[:HID] + t[HID:]

    def stage_b(buf):
        XHL, YHL, U, DA, AHL, GHL, XN, RS = buf
        for k in range(HID // CH):
            ks = slice(k * CH, (k + 1) * CH)
            kl = slice(HID + k * CH, HID + (k + 1) * CH)
            u = U[ks, :]
            t = 1.0 / (1.0 + (0.3275911 * 0.7071067811865476) * jnp.abs(u))
            e = jnp.exp(-0.5 * (u * u))
            poly = t * (0.5 * 0.254829592 + t * (0.5 * -0.284496736 + t * (0.5 * 1.421413741 + t * (0.5 * -1.453152027 + t * (0.5 * 1.061405429)))))
            q = poly * e
            phi = jnp.where(u >= 0.0, 1.0 - q, q)
            g = phi + (0.3989422804014327 * u) * e
            hi, lo = split(u * phi)
            AHL[ks, :] = hi
            AHL[kl, :] = lo
            hi, lo = split(DA[ks, :] * g)
            GHL[ks, :] = hi
            GHL[kl, :] = lo

    def stage_c(i, buf):
        XHL, YHL, U, DA, AHL, GHL, XN, RS = buf
        y = dot(dn3_ref[:, : 2 * HID], AHL[...]) + dot(dn3_ref[:, 2 * HID :], AHL[0:HID, :])
        for q in range(2):
            h = 2 * i + q
            OUT[pl.ds(h, C, stride=H), :] = fmc * (F[h + 3] + (y[:, q * W : (q + 1) * W] + pb_ref[4]))
        t = dot(YHL[...], AHL[0:HID, :], NT)
        GS[...] += t[:C] + (t[C:] + dot(YHL[0:C, :], AHL[HID:, :], NT))
        t = dot(XHL[...], GHL[0:HID, :], NT)
        GE[...] += t[:XR] + (t[XR:] + dot(XHL[0:XR, :], GHL[HID:, :], NT))
        dx = dot(upn3_ref[:, : 2 * HID], GHL[...]) + dot(upn3_ref[:, 2 * HID :], GHL[0:HID, :])
        for q in range(2):
            h = 2 * i + q
            d = dx[:, q * W : (q + 1) * W]
            xn = XN[q]
            ACC[0] += d * xn
            ACC[1] += d
            d = d * pb_ref[2]
            m1 = jnp.mean(d, axis=0, keepdims=True)
            m2 = jnp.mean(d * xn, axis=0, keepdims=True)
            d = (d - m1 - xn * m2) * RS[q, 0:1, :]
            D[h] = d
            ACC[2] += d
            hi, lo = split(d)
            hs = pl.ds(pl.multiple_of(h * C, C), C)
            FHL[hs, 0:W] = hi
            FHL[hs, W:] = lo

    def tiles(i, _):
        b0, b1 = lanesets
        stage_a(2 * i, b0)
        stage_a(2 * i + 1, b1)
        stage_b(b0)
        stage_c(2 * i, b0)
        stage_b(b1)
        stage_c(2 * i + 1, b1)
        return 0

    cot_copy.wait()
    lax.fori_loop(0, H // 4, tiles, 0)
    out_copy = pltpu.make_async_copy(OUT, out_hbm, out_sem)
    out_copy.start()

    def put_gradient(n, rs, y):
        DSH[n, rs, :] = y

    def shift_gradient():
        shift_rows(4 * C, 4, put_gradient)

    def slot(v):
        return v // 48, v % 48 // 3, v % 3

    v = 0
    for j in range(3):
        for i in range(13):
            G[slot(v)] = GE[8 * i : 8 * i + 8, W * j : W * j + W]
            v += 1
    for j in range(3):
        for i in range(12):
            G[slot(v)] = GS[8 * i : 8 * i + 8, W * j : W * j + W]
            v += 1
    while v < SLOTS:
        G[slot(v)] = jnp.zeros((8, W), f32)
        v += 1

    def rdma(src, dst, send, recv, to):
        return pltpu.make_async_remote_copy(
            src_ref=src, dst_ref=dst, send_sem=send, recv_sem=recv, device_id=to, device_id_type=MESH)

    sibling = (gy + 1 - 2 * core, gx)

    def c0():
        return rdma(G.at[1 - core], R0, s0, r0, sibling)

    def c1(i):
        m = (plane + i) & 15
        return rdma(B0.at[m], R1.at[i], s1.at[i], r1.at[i], at_plane(m, core))

    def c2(i):
        return rdma(B1, R2.at[z], s2.at[i], r2.at[i], at_z((z + i) & 7))

    def g2(i):
        j = (z - i) & 7
        return rdma(B1, R2.at[j], s2.at[i], r2.at[i], at_z(j))

    def c3(i):
        ref = sum_ref.at[core, plane]
        return rdma(ref, ref, s3.at[i], r3.at[i], at_plane((plane + i) & 15, core))

    def g3(i):
        m = (plane - i) & 15
        ref = sum_ref.at[core, m]
        return rdma(ref, ref, s3.at[i], r3.at[i], at_plane(m, core))

    def c4():
        ref = sum_ref.at[core]
        return rdma(ref, ref, s4, r4, sibling)

    def g4():
        ref = sum_ref.at[1 - core]
        return rdma(ref, ref, s4, r4, sibling)

    def step(k):
        if k == 0:
            c0().start()
        elif k == 1:
            c0().wait_recv()
            B0[...] = G[core] + R0[...]
            each(1, 16, lambda i: c1(i).start())
        elif k == 2:
            each(1, 16, lambda i: c1(i).wait_recv())
            acc = B0[plane]
            for i in range(1, 16):
                acc = acc + R1[i]
            B1[...] = acc
            R2[z] = acc
            each(1, 8, lambda i: c2(i).start())
        elif k == 3:
            each(1, 8, lambda i: g2(i).wait_recv())
            acc = R2[0]
            for j in range(1, 8):
                acc = acc + R2[j]
            sum_ref[core, plane] = acc
            each(1, 16, lambda i: c3(i).start())
        elif k == 4:
            each(1, 16, lambda i: g3(i).wait_recv())
            c4().start()
        else:
            g4().wait_recv()
            c0().wait_send()
            each(1, 16, lambda i: c1(i).wait_send())
            each(1, 8, lambda i: c2(i).wait_send())
            each(1, 16, lambda i: c3(i).wait_send())
            c4().wait_send()

    right = (pos >= 3) & (pos < 6)

    def back_block(cb, _):
        for k, when in enumerate(STEPS):
            @pl.when(cb == when)
            def _(k=k):
                step(k + 1)

        cs = pl.ds(pl.multiple_of(cb * 8, 8), 8)
        packed = jnp.zeros((8, W), f32)
        for h in range(H):
            packed = jnp.where(prow == h, roll(D[h, cs, :], 8 * h + 3), packed)
        packed = jnp.where(left, roll(packed, -3), jnp.where(right, roll(packed, 3), 0.0))
        vs = [packed]
        for k in (1, 2):
            vs.append(jnp.where(left, jnp.where(pos >= k, roll(packed, k), 0.0),
                                jnp.where(right & (pos < 6 - k), roll(packed, -k), 0.0)))
        fs0 = FS[0, cs, :]
        fs1 = FS[1, cs, :]
        o0 = jnp.zeros((8, W), f32)
        o1 = jnp.zeros((8, W), f32)
        spill = {}
        for a in range(7):
            win = jnp.where(prow < 11 - a, roll(fs0, -8 * a), roll(fs1, 8 * (11 - a)))
            t = None
            for k in range(3):
                w = wbs_ref[cb, 3 * a + k]
                t = w * vs[k] if t is None else t + w * vs[k]
                x = vs[k] * win
                spill[a, k] = jnp.where(left, x, 0.0)
                spill[a, 6 - k] = jnp.where(left, 0.0, x)
            o0 = o0 + jnp.where((prow >= a) & (prow < 11), roll(t, 8 * a), 0.0)
            o1 = o1 + jnp.where(prow < 5 + a, roll(t, 8 * (a - 11)), 0.0)
        o0 = o0 * ok0
        o1 = o1 * ok1
        DFS[0, cs, :] = o0
        DFS[1, cs, :] = o1

        def gradient_rows(b):
            if b == 3:
                return [D[h, cs, :] for h in range(H)]
            n = SHIFTS.index(6 - b)
            return [DSH[n, pl.ds(pl.multiple_of(h * C + cb * 8, 8), 8), :] for h in range(H)]

        grads = jnp.zeros((8, W), f32)
        rows = [F[r, cs, :] for r in range(EXT)]
        for b in range(7):
            dd = gradient_rows(b)
            for a in range(7):
                part = spill.get((a, b))
                for h in range(H):
                    t = dd[h] * rows[h + a]
                    part = t if part is None else part + t
                total = jnp.sum(part, axis=1, keepdims=True)
                grads = jnp.where(lane == 7 * a + b, total, grads)
        acc = [DY[r - 3, cs, :] if 3 <= r < H + 3 else None for r in range(EXT)]
        for b in range(7):
            dd = gradient_rows(b)
            for a in range(7):
                w = wb_ref[cb, 7 * a + b]
                for h in range(H):
                    t = w * dd[h]
                    acc[h + a] = t if acc[h + a] is None else acc[h + a] + t
        for k, src in enumerate((2, 0, 1, 3)):
            total = jnp.sum(ACC[src, cs, :], axis=1, keepdims=True)
            grads = jnp.where(lane == DEPTH_B + k, total, grads)
        total = o0 + o1
        for r in range(EXT):
            t = acc[r]
            if r < 3:
                t = t * top_ok
            elif r >= H + 3:
                t = t * bot_ok
            DF[r, cs, :] = t
            total = total + t
        total = jnp.sum(total, axis=1, keepdims=True)
        GV[cs, :] = jnp.where(lane == STEM_B, total, grads)
        return 0

    step(0)
    shift_gradient()
    lax.fori_loop(0, NB, back_block, 0)
    step(len(STEPS) + 1)

    def rows2(p0, p1, d0, d1):
        ph, plo = split(jnp.concatenate([p0, p1], axis=1))
        dh, dlo = split(jnp.concatenate([d0, d1], axis=1))
        t = dot(jnp.concatenate([ph, plo], axis=0), dh, NT)
        return t[:KK] + (t[KK:] + dot(ph, dlo, NT))

    def okpat(p, ok):
        return p if ok is None else jnp.where(ok > 0.0, p, 0.0)

    def row_ok(r):
        return top_ok if r < 3 else bot_ok if r >= H + 3 else None

    okk = [jnp.concatenate([ok] * (KK // 8), axis=0) for ok in (ok0, ok1)]
    gstem = rows2(okpat(side_ref[0], okk[0]), okpat(side_ref[1], okk[1]), DFS[0], DFS[1])
    for r in range(0, EXT, 2):
        gstem = gstem + rows2(
            okpat(pat_ref[r], row_ok(r)), okpat(pat_ref[r + 1], row_ok(r + 1)), DF[r], DF[r + 1])

    zero = jnp.zeros((KK, W - C), f32)
    gs = jnp.concatenate([gstem, zero], axis=1)
    vec = jnp.concatenate([GV[...], jnp.zeros((W - C, W), f32)], axis=0).T
    tail = [gs[8 * i : 8 * i + 8, :] for i in range(6)] + [vec[8 * i : 8 * i + 8, :] for i in range(7)]
    for i, v in enumerate(tail):
        TG[i] = v
    for i in range(len(tail), TAIL):
        TG[i] = jnp.zeros((8, W), f32)

    def owner(v):
        return at_plane(v, v & 1)

    mine = (plane & 1) == core

    def t1(v):
        return rdma(TG.at[v], TR.at[plane, core], ts1.at[v], tr1.at[plane, core], owner(v))

    def w1(m, c):
        return rdma(TP, TR.at[m, c], ts1.at[0], tr1.at[m, c], at_plane(m, c))

    def t2(i):
        return rdma(TP, TX.at[z], ts2.at[i], tr2.at[i], at_z((z + i) & 7))

    def w2(i):
        j = (z - i) & 7
        return rdma(TP, TX.at[j], ts2.at[i], tr2.at[i], at_z(j))

    def t3(m, c):
        ref = tail_ref.at[plane]
        return rdma(ref, ref, ts3.at[m, c], tr3.at[plane], at_plane(m, c))

    def w3(v):
        ref = tail_ref.at[v]
        return rdma(ref, ref, ts3.at[0, 0], tr3.at[v], owner(v))

    def others(f):
        def one(i):
            m, c = i >> 1, i & 1
            @pl.when((m != plane) | (c != core))
            def _():
                f(m, c)
        each(0, 32, one)

    def foreign(f):
        def one(v):
            @pl.when((v != plane) | ((v & 1) != core))
            def _():
                f(v)
        each(0, TAIL, one)

    foreign(lambda v: t1(v).start())

    @pl.when(mine)
    def _():
        TR[plane, core] = TG[plane]
        others(lambda m, c: w1(m, c).wait_recv())
        acc = TR[0, 0]
        for i in range(1, 32):
            acc = acc + TR[i >> 1, i & 1]
        TP[...] = acc
        TX[z] = acc
        each(1, 8, lambda i: t2(i).start())

    step(len(STEPS) + 2)

    @pl.when(mine)
    def _():
        each(1, 8, lambda i: w2(i).wait_recv())
        acc = TX[0]
        for j in range(1, 8):
            acc = acc + TX[j]
        tail_ref[plane] = acc
        others(lambda m, c: t3(m, c).start())

    step(len(STEPS) + 3)
    foreign(lambda v: t1(v).wait_send())
    step(len(STEPS) + 4)
    foreign(lambda v: w3(v).wait_recv())

    @pl.when(mine)
    def _():
        each(1, 8, lambda i: t2(i).wait_send())
        others(lambda m, c: t3(m, c).wait_send())

    out_copy.wait()
    for group in range(len(GROUPS)):
        for bucket_at in range(2):
            tile_copy(bucket_at, group).wait_send()
    row_copy(True).wait_send()
    row_copy(False).wait_send()
    for i in range(len(NEAR)):
        edge_copy(i).wait_send()
    for group in (1, 2):
        for i in range(2):
            mid_copy(group, i).wait_send()


def whole_call(*args):
    vm = pl.BlockSpec(memory_space=pltpu.VMEM)
    hbm = pl.BlockSpec(memory_space=pltpu.HBM)
    s = jax.ShapeDtypeStruct
    n_send = INFO + 3 * H
    near = len(NEAR)

    def v(*shape, dtype=f32):
        return pltpu.VMEM(shape, dtype)

    buf = [
        v(2 * XR, 2 * W, dtype=bf16), v(2 * C, 2 * W, dtype=bf16), v(HID, 2 * W), v(HID, 2 * W),
        v(2 * HID, 2 * W, dtype=bf16), v(2 * HID, 2 * W, dtype=bf16), v(2, C, W), v(2, 8, W),
    ]
    return pl.pallas_call(
        whole_kernel,
        out_shape=(s((C * H, W), f32), s((2, 16, 3, 8, W), f32), s((TAIL, 8, W), f32)),
        in_specs=[hbm] * 14,
        out_specs=[hbm, vm, vm],
        scratch_shapes=[
            v(EXT, KK, W), v(2, KK, W), v(8, W), v(NB, TAPS, 8, W), v(NB, 21, 8, W), v(5, C, W),
            v(C, 3 * KK, dtype=bf16), v(2 * HID, 2 * XR, dtype=bf16), v(2 * HID, 2 * C, dtype=bf16),
            v(C, 3 * HID, dtype=bf16), v(C, 3 * HID, dtype=bf16),
            v(8, PIX), v(1, 8, dtype=jnp.int32), v(1, 8, dtype=jnp.int32),
            v(KK, C), v(TAPS, C), v(1, C), v(1, C), v(1, C), v(1, C), v(C, HID), v(1, HID), v(C, HID), v(1, C),
            v(2, n_send, 8, W), v(2, n_send, 8, W), v(3, KK, W), v(near, KK, W), v(2, 2, KK, W), v(W, W), v(C * H, W),
            DMA((12,)), DMA((12,)), DMA((2, 3)), DMA((2, 3)), DMA((2,)), DMA((2,)),
            DMA((near,)), DMA((near,)), DMA((2, 2)), DMA((2, 2)), DMA(()), DMA(()),
            v(EXT, C, W), v(2, C, W), v(H, C, W), v(6, H * C, W), v(H, C, W), v(XR, HID), v(C, HID), v(4, C, W),
            v(EXT * C, 2 * W, dtype=bf16), v(6, EXT * C, W), v(2 * W, 6 * W, dtype=bf16), v(C * H, W),
            v(2, 16, 3, 8, W), v(16, 3, 8, W), v(16, 3, 8, W), v(16, 3, 8, W), v(3, 8, W), v(8, 3, 8, W),
            v(TAIL, 8, W), v(16, 2, 8, W), v(8, W), v(8, 8, W), v(EXT, C, W), v(2, C, W), v(C, W),
            DMA(()), DMA(()), DMA((16,)), DMA((16,)), DMA((8,)), DMA((8,)), DMA((16,)), DMA((16,)), DMA(()), DMA(()),
            DMA((TAIL,)), DMA((16, 2)), DMA((8,)), DMA((8,)), DMA((16, 2)), DMA((TAIL,)),
            *buf, *buf,
        ],
        compiler_params=pltpu.CompilerParams(
            collective_id=0, has_side_effects=True, vmem_limit_bytes=56 * 1024 * 1024),
        name="whole",
    )(*args)


def unpack_kernel(
    sum_ref, tail_ref, block_hbm, out_hbm, gstem_ref, gstem_b_ref, gdepth_ref, gdepth_b_ref, ggain_ref, gnbias_ref,
    gexp_ref, gexp_b_ref, gshr_ref, gshr_b_ref, held, sem,
):
    into = pltpu.make_async_copy(block_hbm, held, sem.at[0])
    into.start()

    def at(v):
        return sum_ref[v // 48, v % 48 // 3, v % 3]

    v = 0
    for j in range(3):
        for i in range(12):
            gexp_ref[8 * i : 8 * i + 8, W * j : W * j + W] = at(v)
            v += 1
        gexp_b_ref[:, W * j : W * j + W] = at(v)[0:1, :]
        v += 1
    for j in range(3):
        for i in range(12):
            gshr_ref[8 * i : 8 * i + 8, W * j : W * j + W] = at(v)
            v += 1
    into.wait()
    back = pltpu.make_async_copy(held, out_hbm, sem.at[1])
    back.start()
    for i in range(6):
        gstem_ref[8 * i : 8 * i + 8, :] = tail_ref[i][:, :C]
        gdepth_ref[8 * i : 8 * i + 8, :] = tail_ref[6 + i][:, :C]
    last = tail_ref[12][:, :C]
    gdepth_ref[48:49, :] = last[0:1]
    for k, ref in enumerate((gstem_b_ref, gdepth_b_ref, ggain_ref, gnbias_ref, gshr_b_ref)):
        ref[...] = last[k + 1 : k + 2]
    back.wait()


def unpack_call(block, total, tail):
    vm = pl.BlockSpec(memory_space=pltpu.VMEM)
    hbm = pl.BlockSpec(memory_space=pltpu.HBM)
    shapes = ((KK, C), (1, C), (TAPS, C), (1, C), (1, C), (1, C), (C, HID), (1, HID), (C, HID), (1, C))
    return pl.pallas_call(
        unpack_kernel,
        out_shape=tuple(jax.ShapeDtypeStruct(s, f32) for s in ((C * H, W),) + shapes),
        in_specs=[vm, vm, hbm],
        out_specs=[hbm] + [vm] * len(shapes),
        scratch_shapes=[pltpu.VMEM((C * H, W), f32), DMA((2,))],
        compiler_params=pltpu.CompilerParams(vmem_limit_bytes=56 * 1024 * 1024),
        name="unpack",
    )(total, tail, block)


def local(
    stored_tiles, tile_target, tile_mask,
    stem_weight, stem_bias, depth_weight, depth_bias, norm_gain, norm_bias,
    expand_weight, expand_bias, shrink_weight, shrink_bias, cotangent,
):
    def row(v):
        return v.reshape(1, -1)

    block, total, tail = whole_call(
        stored_tiles[0], tile_target, tile_mask, stem_weight, depth_weight, row(stem_bias), row(depth_bias),
        row(norm_gain), row(norm_bias), expand_weight, row(expand_bias), shrink_weight.T, row(shrink_bias),
        cotangent.reshape(C * H, W))
    out, gs, gsb, gd, gdb, gg, gn, ge, geb, gh, ghb = unpack_call(block, total, tail)
    return (
        out.reshape(C, H, W), gs, gsb[0], gd, gdb[0], gg[0], gn[0], ge, geb[0], gh.T, ghb[0],
    )


def solution(mesh):
    placed = (P("gy", "gx", None), P("gy", "gx"), P("gy", "gx")) + (P(),) * 10 + (P(None, "gy", "gx"),)
    return jax.shard_map(
        local, mesh=mesh, in_specs=placed,
        out_specs=(P(None, "gy", "gx"),) + (P(),) * 10,
        check_vma=False,
    )
```

profile of v0, /device:TPU:1, one launch (start us, length us, event | category | flops | bytes accessed | tf_op | source)
XLA Modules:
  0.0 82.0 jit_solution(12740800328252575127)
XLA Ops:
  0.6 0.0 copy-start
  0.7 0.7 copy-done
  1.3 0.6 reshape.50.eb_hbm
  1.9 75.0 %whole.1 = (f32[1536,128]{1,0:T(8,128)}, f32[2,16,3,8,128]{4,3,2,1,0:T(8,128)}, f32[16,8,128]{2,1,0:T(8,128)}) custom-call(f32[8,12288]{1,0:T(8,128)} %bitcast.16, s32[1,8]{1,0:T(1,128)} %target_hbm.1, s32[1,8]{1,0:T(1,128)} %marks_hbm.1, f32[48,96]{1,0:T(8,128)} %stem_hbm.1, f32[49,96]{1,0:T(8,128)} %dw_hbm.1, f32[1,96]{1,0:T(1,128)} %bitcast.18, ...), custom_call_target="tpu_custom_call" | custom-call | tf_op jit(solution)/shard_map/whole/pallas_call | solution.py:882
  76.9 3.8 %unpack.1 = (f32[1536,128]{1,0:T(8,128)}, f32[48,96]{1,0:T(8,128)}, f32[1,96]{1,0:T(1,128)}, f32[49,96]{1,0:T(8,128)}, f32[1,96]{1,0:T(1,128)}, /*index=5*/f32[1...) custom-call(f32[2,16,3,8,128]{4,3,2,1,0:T(8,128)} %get-tuple-element, ...), custom_call_target="tpu_custom_call" | custom-call | tf_op jit(solution)/shard_map/unpack/pallas_call | solution.py:948
  80.7 0.0 copy-start.1
  80.7 0.7 copy-done.1
  81.4 0.6 reduce
Async XLA Ops:
  0.6 0.7 copy-start
  80.7 0.7 copy-start.1
where the time goes:
time: 82.2 us; the launch traced here: 82 us
  Pallas kernels  78.8 us (96%)
  local copies, waits for them, and re-layouts  1.91 us (2%)
    pallas_call x1, Pallas kernels, whole_call(): pl.pallas_call(whole_kernel, out_shape=(s((C * H, W), f32), s((2, 16, 3,...  75 us
    pallas_call x1, Pallas kernels, unpack_call(): pl.pallas_call(unpack_kernel, out_shape=tuple((jax.ShapeDtypeStruct(s, f3...  3.78 us

commit v1 on v0

--- a/solution.py
+++ b/solution.py
@@ -73,7 +73,7 @@
     lax.fori_loop(low, high, one, 0)
 
 
-XR = C + 16
+XR = W
 CH = 16
 SLOTS = 96
 TAIL = 16
@@ -104,7 +104,7 @@
     target, marks, stem_v, dw_v, sb_v, db_v, ga_v, nb_v, ew_v, eb_v, sw_v, hb_v, send, recv, edge, edges,
     edges_mid, ct, cot_ref, in_sem, par_sem, tile_send, tile_recv, row_send, row_recv, edge_send, edge_recv,
     mid_send, mid_recv, cot_sem, out_sem, F, FS, D, DSH, DY, GE, GS, ACC, FHL, FSH, SH, OUT, G, R0, B0, R1, B1,
-    R2, TG, TR, TP, TX, DF, DFS, GV, s0, r0, s1, r1, s2, r2, s3, r3, s4, r4, ts1, tr1, ts2, tr2, ts3, tr3, *bufs,
+    R2, TG, TR, TP, TX, DF, DFS, GV, s0, r0, s1, r1, s2, r2, s3, r3, s4, r4, ts1, tr1, ts2, tr2, ts3, tr3, HALO, SPX, *bufs,
 ):
     gy = lax.axis_index("gy")
     gx = lax.axis_index("gx")
@@ -230,9 +230,9 @@
                 for b in range(7):
                     t = 7 * a + b
                     taps.append(jnp.broadcast_to(wc[:, t : t + 1], (8, W)))
-                    wb_ref[cb, t] = taps[-1]
+                    wb_ref[t, cs, :] = taps[-1]
                 for k in range(3):
-                    wbs_ref[cb, 3 * a + k] = jnp.where(left, taps[k], taps[6 - k])
+                    wbs_ref[3 * a + k, cs, :] = jnp.where(left, taps[k], taps[6 - k])
             for k in range(5):
                 pb_ref[k, cs, :] = jnp.broadcast_to(wc[:, STEM_B + k : STEM_B + k + 1], (8, W))
             return 0
@@ -257,15 +257,17 @@
             ref[:, 2 * HID :] = lo
         hi, lo = split(turned_over(sw)[:, :C])
         dnn2_ref[0:HID, 0:C] = hi
-        dnn2_ref[0:HID, C : 2 * C] = hi
+        dnn2_ref[0:HID, W : W + C] = hi
         dnn2_ref[HID:, 0:C] = lo
-        dnn2_ref[HID:, C : 2 * C] = jnp.zeros((HID, C), bf16)
-        up = jnp.concatenate([ew, eb_v[...], jnp.zeros((W - C - 1, HID), f32)], axis=0).T
-        hi, lo = split(up[:, : C + 16])
-        up2_ref[0:HID, 0 : C + 16] = hi
-        up2_ref[0:HID, C + 16 :] = hi
-        up2_ref[HID:, 0 : C + 16] = lo
-        up2_ref[HID:, C + 16 :] = jnp.zeros((HID, C + 16), bf16)
+        dnn2_ref[HID:, W:] = jnp.zeros((HID, W), bf16)
+        dnn2_ref[:, C:W] = jnp.zeros((2 * HID, W - C), bf16)
+        dnn2_ref[0:HID, W + C :] = jnp.zeros((HID, W - C), bf16)
+        up = jnp.concatenate([ew, eb_v[...].reshape(1, HID), jnp.zeros((W - C - 1, HID), f32)], axis=0).T
+        hi, lo = split(up[:, : W])
+        up2_ref[0:HID, 0 : W] = hi
+        up2_ref[0:HID, W :] = hi
+        up2_ref[HID:, 0 : W] = lo
+        up2_ref[HID:, W :] = jnp.zeros((HID, W), bf16)
 
 
     put(0, place_col, place_col)
@@ -421,52 +423,49 @@
     for i, ok in enumerate((ok0, ok1)):
         FS[i] = y[:, i * W : (i + 1) * W] * jnp.concatenate([ok] * NB, axis=0)
 
-    def shift_rows(rows, count, put):
+    def shift_rows(ref, starts, rows):
         for n in range(3):
-            def some(i, _, n=n):
-                rs = pl.ds(pl.multiple_of(i * rows, rows), rows)
-                y = dot(FHL[rs, :], SH[:, 2 * n * W : (2 * n + 2) * W])
-                put(2 * n, rs, y[:, :W])
-                put(2 * n + 1, rs, y[:, W:])
-                return 0
-            lax.fori_loop(0, count, some, 0)
-
-    def put_features(n, rs, y):
-        FSH[n, rs, :] = y
-
-    shift_rows(4 * C, 5, put_features)
-    for n in range(3):
-        rs = slice(20 * C, 22 * C)
-        y = dot(FHL[rs, :], SH[:, 2 * n * W : (2 * n + 2) * W])
-        FSH[2 * n, rs, :] = y[:, :W]
-        FSH[2 * n + 1, rs, :] = y[:, W:]
-
-    edge_lane = (lane < 3) | (lane >= W - 3)
+            for at in starts:
+                y = dot(FHL[at : at + rows, :], SH[:, 2 * n * W : (2 * n + 2) * W])
+                for r in range(rows // C):
+                    ref[2 * n, at // C + r] = y[r * C : (r + 1) * C, :W]
+                    ref[2 * n + 1, at // C + r] = y[r * C : (r + 1) * C, W:]
+
+    shift_rows(FSH, (0, 11 * C), 11 * C)
+
+    def window(a, lo, hi):
+        return jnp.where(prow96 < 11 - a, roll(lo, -8 * a), roll(hi, 8 * (11 - a)))
+
+    lane96 = lanes((C, W))
+    pos96 = lane96 & 7
+    prow96 = lane96 >> 3
+    left96 = pos96 < 3
+    right96 = (pos96 >= 3) & (pos96 < 6)
+    edge96 = (lane96 < 3) | (lane96 >= W - 3)
+    part = [None] * 3
+    for a in range(7):
+        win = window(a, FS[0], FS[1])
+        for k in range(3):
+            t = wbs_ref[3 * a + k] * win
+            part[k] = t if part[k] is None else part[k] + t
+    q = part[0]
+    for k in (1, 2):
+        q = q + jnp.where(left96, jnp.where(pos96 < 3 - k, roll(part[k], -k), 0.0),
+                          jnp.where((pos96 >= 3 + k) & (pos96 < 6), roll(part[k], k), 0.0))
+    q = jnp.where(left96, roll(q, -3), roll(q, 3))
+    for h in range(H):
+        HALO[h] = pb_ref[1] + jnp.where(edge96, roll(q, 125 - 8 * h), 0.0)
 
     def conv_block(cb, _):
         cs = pl.ds(pl.multiple_of(cb * 8, 8), 8)
-        part = [None] * 3
-        fs0 = FS[0, cs, :]
-        fs1 = FS[1, cs, :]
-        for a in range(7):
-            win = jnp.where(prow < 11 - a, roll(fs0, -8 * a), roll(fs1, 8 * (11 - a)))
-            for k in range(3):
-                t = wbs_ref[cb, 3 * a + k] * win
-                part[k] = t if part[k] is None else part[k] + t
-        q = part[0]
-        for k in (1, 2):
-            q = q + jnp.where(left, jnp.where(pos < 3 - k, roll(part[k], -k), 0.0),
-                              jnp.where((pos >= 3 + k) & (pos < 6), roll(part[k], k), 0.0))
-        q = jnp.where(left, roll(q, -3), roll(q, 3))
-        bias = pb_ref[1, cs, :]
-        acc = [bias + jnp.where(edge_lane, roll(q, 125 - 8 * h), 0.0) for h in range(H)]
+        acc = [HALO[h, cs, :] for h in range(H)]
         for b in range(7):
             if b == 3:
                 rows = [F[r, cs, :] for r in range(EXT)]
             else:
-                rows = [FSH[SHIFTS.index(b), pl.ds(pl.multiple_of(r * C + cb * 8, 8), 8), :] for r in range(EXT)]
+                rows = [FSH[SHIFTS.index(b), r, cs, :] for r in range(EXT)]
             for a in range(7):
-                w = wb_ref[cb, 7 * a + b]
+                w = wb_ref[7 * a + b, cs, :]
                 for h in range(H):
                     acc[h] = acc[h] + w * rows[h + a]
         for h in range(H):
@@ -476,11 +475,14 @@
     lax.fori_loop(0, NB, conv_block, 0)
 
     fmc = jnp.concatenate([fm_ref[...]] * NB, axis=0)
-    ones_row = jnp.where(lax.broadcasted_iota(jnp.int32, (16, 2 * W), 0) == 0, 1.0, 0.0)
+    ones_row = jnp.where(lax.broadcasted_iota(jnp.int32, (W - C, 2 * W), 0) == 0, 1.0, 0.0)
     lanesets = [bufs[: len(bufs) // 2], bufs[len(bufs) // 2 :]]
-    for XHL, *_ in lanesets:
+    none = jnp.zeros((W - C, 2 * W), bf16)
+    for XHL, YHL, *_ in lanesets:
+        YHL[C:W, :] = none
+        YHL[W + C :, :] = none
         XHL[C:XR, :] = ones_row.astype(bf16)
-        XHL[XR + C :, :] = jnp.zeros((16, 2 * W), bf16)
+        XHL[XR + C :, :] = none
     GE[...] = jnp.zeros_like(GE)
     GS[...] = jnp.zeros_like(GS)
     ACC[...] = jnp.zeros_like(ACC)
@@ -506,7 +508,7 @@
             ACC[3] += dy
             hi, lo = split(dy)
             YHL[0:C, qs] = hi
-            YHL[C:, qs] = lo
+            YHL[W : W + C, qs] = lo
         t = dot(up2_ref[...], XHL[...])
         U[...] = t[:HID] + t[HID:]
         t = dot(dnn2_ref[...], YHL[...])
@@ -518,8 +520,10 @@
             ks = slice(k * CH, (k + 1) * CH)
             kl = slice(HID + k * CH, HID + (k + 1) * CH)
             u = U[ks, :]
-            t = 1.0 / (1.0 + (0.3275911 * 0.7071067811865476) * jnp.abs(u))
-            e = jnp.exp(-0.5 * (u * u))
+            x = 1.0 + (0.3275911 * 0.7071067811865476) * jnp.abs(u)
+            t = pl.reciprocal(x, approx=True)
+            t = t * (2.0 - x * t)
+            e = jnp.exp2(-0.7213475204444817 * (u * u))
             poly = t * (0.5 * 0.254829592 + t * (0.5 * -0.284496736 + t * (0.5 * 1.421413741 + t * (0.5 * -1.453152027 + t * (0.5 * 1.061405429)))))
             q = poly * e
             phi = jnp.where(u >= 0.0, 1.0 - q, q)
@@ -537,10 +541,9 @@
         for q in range(2):
             h = 2 * i + q
             OUT[pl.ds(h, C, stride=H), :] = fmc * (F[h + 3] + (y[:, q * W : (q + 1) * W] + pb_ref[4]))
-        t = dot(YHL[...], AHL[0:HID, :], NT)
-        GS[...] += t[:C] + (t[C:] + dot(YHL[0:C, :], AHL[HID:, :], NT))
-        t = dot(XHL[...], GHL[0:HID, :], NT)
-        GE[...] += t[:XR] + (t[XR:] + dot(XHL[0:XR, :], GHL[HID:, :], NT))
+        for total, wide, tall in ((GS, YHL, AHL), (GE, XHL, GHL)):
+            t = dot(tall[0:HID, :], wide[...], NT)
+            total[...] += t[:, :W] + (t[:, W:] + dot(tall[HID:, :], wide[0:W, :], NT))
         dx = dot(upn3_ref[:, : 2 * HID], GHL[...]) + dot(upn3_ref[:, 2 * HID :], GHL[0:HID, :])
         for q in range(2):
             h = 2 * i + q
@@ -574,24 +577,19 @@
     out_copy = pltpu.make_async_copy(OUT, out_hbm, out_sem)
     out_copy.start()
 
-    def put_gradient(n, rs, y):
-        DSH[n, rs, :] = y
-
     def shift_gradient():
-        shift_rows(4 * C, 4, put_gradient)
+        shift_rows(DSH, (0, 8 * C), 8 * C)
 
     def slot(v):
         return v // 48, v % 48 // 3, v % 3
 
     v = 0
-    for j in range(3):
-        for i in range(13):
-            G[slot(v)] = GE[8 * i : 8 * i + 8, W * j : W * j + W]
-            v += 1
-    for j in range(3):
-        for i in range(12):
-            G[slot(v)] = GS[8 * i : 8 * i + 8, W * j : W * j + W]
-            v += 1
+    for total, count in ((GE, 13), (GS, 12)):
+        for j in range(3):
+            t = total[W * j : W * j + W, :].T
+            for i in range(count):
+                G[slot(v)] = t[8 * i : 8 * i + 8, :]
+                v += 1
     while v < SLOTS:
         G[slot(v)] = jnp.zeros((8, W), f32)
         v += 1
@@ -666,7 +664,6 @@
             each(1, 16, lambda i: c3(i).wait_send())
             c4().wait_send()
 
-    right = (pos >= 3) & (pos < 6)
 
     def back_block(cb, _):
         for k, when in enumerate(STEPS):
@@ -675,47 +672,23 @@
                 step(k + 1)
 
         cs = pl.ds(pl.multiple_of(cb * 8, 8), 8)
-        packed = jnp.zeros((8, W), f32)
-        for h in range(H):
-            packed = jnp.where(prow == h, roll(D[h, cs, :], 8 * h + 3), packed)
-        packed = jnp.where(left, roll(packed, -3), jnp.where(right, roll(packed, 3), 0.0))
-        vs = [packed]
-        for k in (1, 2):
-            vs.append(jnp.where(left, jnp.where(pos >= k, roll(packed, k), 0.0),
-                                jnp.where(right & (pos < 6 - k), roll(packed, -k), 0.0)))
-        fs0 = FS[0, cs, :]
-        fs1 = FS[1, cs, :]
-        o0 = jnp.zeros((8, W), f32)
-        o1 = jnp.zeros((8, W), f32)
-        spill = {}
-        for a in range(7):
-            win = jnp.where(prow < 11 - a, roll(fs0, -8 * a), roll(fs1, 8 * (11 - a)))
-            t = None
-            for k in range(3):
-                w = wbs_ref[cb, 3 * a + k]
-                t = w * vs[k] if t is None else t + w * vs[k]
-                x = vs[k] * win
-                spill[a, k] = jnp.where(left, x, 0.0)
-                spill[a, 6 - k] = jnp.where(left, 0.0, x)
-            o0 = o0 + jnp.where((prow >= a) & (prow < 11), roll(t, 8 * a), 0.0)
-            o1 = o1 + jnp.where(prow < 5 + a, roll(t, 8 * (a - 11)), 0.0)
-        o0 = o0 * ok0
-        o1 = o1 * ok1
-        DFS[0, cs, :] = o0
-        DFS[1, cs, :] = o1
-
         def gradient_rows(b):
             if b == 3:
                 return [D[h, cs, :] for h in range(H)]
             n = SHIFTS.index(6 - b)
-            return [DSH[n, pl.ds(pl.multiple_of(h * C + cb * 8, 8), 8), :] for h in range(H)]
+            return [DSH[n, h, cs, :] for h in range(H)]
 
         grads = jnp.zeros((8, W), f32)
         rows = [F[r, cs, :] for r in range(EXT)]
         for b in range(7):
             dd = gradient_rows(b)
             for a in range(7):
-                part = spill.get((a, b))
+                if b == 3:
+                    part = None
+                elif b < 3:
+                    part = jnp.where(left, SPX[3 * a + b, cs, :], 0.0)
+                else:
+                    part = jnp.where(left, 0.0, SPX[3 * a + 6 - b, cs, :])
                 for h in range(H):
                     t = dd[h] * rows[h + a]
                     part = t if part is None else part + t
@@ -725,14 +698,14 @@
         for b in range(7):
             dd = gradient_rows(b)
             for a in range(7):
-                w = wb_ref[cb, 7 * a + b]
+                w = wb_ref[7 * a + b, cs, :]
                 for h in range(H):
                     t = w * dd[h]
                     acc[h + a] = t if acc[h + a] is None else acc[h + a] + t
         for k, src in enumerate((2, 0, 1, 3)):
             total = jnp.sum(ACC[src, cs, :], axis=1, keepdims=True)
             grads = jnp.where(lane == DEPTH_B + k, total, grads)
-        total = o0 + o1
+        total = DFS[0, cs, :] + DFS[1, cs, :]
         for r in range(EXT):
             t = acc[r]
             if r < 3:
@@ -747,6 +720,29 @@
 
     step(0)
     shift_gradient()
+
+    packed = jnp.zeros((C, W), f32)
+    for h in range(H):
+        packed = jnp.where(prow96 == h, roll(D[h], 8 * h + 3), packed)
+    packed = jnp.where(left96, roll(packed, -3), jnp.where(right96, roll(packed, 3), 0.0))
+    vs = [packed]
+    for k in (1, 2):
+        vs.append(jnp.where(left96, jnp.where(pos96 >= k, roll(packed, k), 0.0),
+                            jnp.where(right96 & (pos96 < 6 - k), roll(packed, -k), 0.0)))
+    o0 = jnp.zeros((C, W), f32)
+    o1 = jnp.zeros((C, W), f32)
+    for a in range(7):
+        win = window(a, FS[0], FS[1])
+        t = None
+        for k in range(3):
+            u = wbs_ref[3 * a + k] * vs[k]
+            t = u if t is None else t + u
+            SPX[3 * a + k] = vs[k] * win
+        o0 = o0 + jnp.where((prow96 >= a) & (prow96 < 11), roll(t, 8 * a), 0.0)
+        o1 = o1 + jnp.where(prow96 < 5 + a, roll(t, 8 * (a - 11)), 0.0)
+    DFS[0] = o0 * jnp.concatenate([ok0] * NB, axis=0)
+    DFS[1] = o1 * jnp.concatenate([ok1] * NB, axis=0)
+
     lax.fori_loop(0, NB, back_block, 0)
     step(len(STEPS) + 1)
 
@@ -876,7 +872,7 @@
         return pltpu.VMEM(shape, dtype)
 
     buf = [
-        v(2 * XR, 2 * W, dtype=bf16), v(2 * C, 2 * W, dtype=bf16), v(HID, 2 * W), v(HID, 2 * W),
+        v(2 * XR, 2 * W, dtype=bf16), v(2 * W, 2 * W, dtype=bf16), v(HID, 2 * W), v(HID, 2 * W),
         v(2 * HID, 2 * W, dtype=bf16), v(2 * HID, 2 * W, dtype=bf16), v(2, C, W), v(2, 8, W),
     ]
     return pl.pallas_call(
@@ -885,20 +881,20 @@
         in_specs=[hbm] * 14,
         out_specs=[hbm, vm, vm],
         scratch_shapes=[
-            v(EXT, KK, W), v(2, KK, W), v(8, W), v(NB, TAPS, 8, W), v(NB, 21, 8, W), v(5, C, W),
-            v(C, 3 * KK, dtype=bf16), v(2 * HID, 2 * XR, dtype=bf16), v(2 * HID, 2 * C, dtype=bf16),
+            v(EXT, KK, W), v(2, KK, W), v(8, W), v(TAPS, C, W), v(21, C, W), v(5, C, W),
+            v(C, 3 * KK, dtype=bf16), v(2 * HID, 2 * XR, dtype=bf16), v(2 * HID, 2 * W, dtype=bf16),
             v(C, 3 * HID, dtype=bf16), v(C, 3 * HID, dtype=bf16),
             v(8, PIX), v(1, 8, dtype=jnp.int32), v(1, 8, dtype=jnp.int32),
-            v(KK, C), v(TAPS, C), v(1, C), v(1, C), v(1, C), v(1, C), v(C, HID), v(1, HID), v(C, HID), v(1, C),
+            v(KK, C), v(TAPS, C), v(1, C), v(1, C), v(1, C), v(1, C), v(C, HID), v(HID), v(C, HID), v(1, C),
             v(2, n_send, 8, W), v(2, n_send, 8, W), v(3, KK, W), v(near, KK, W), v(2, 2, KK, W), v(W, W), v(C * H, W),
             DMA((12,)), DMA((12,)), DMA((2, 3)), DMA((2, 3)), DMA((2,)), DMA((2,)),
             DMA((near,)), DMA((near,)), DMA((2, 2)), DMA((2, 2)), DMA(()), DMA(()),
-            v(EXT, C, W), v(2, C, W), v(H, C, W), v(6, H * C, W), v(H, C, W), v(XR, HID), v(C, HID), v(4, C, W),
-            v(EXT * C, 2 * W, dtype=bf16), v(6, EXT * C, W), v(2 * W, 6 * W, dtype=bf16), v(C * H, W),
+            v(EXT, C, W), v(2, C, W), v(H, C, W), v(6, H, C, W), v(H, C, W), v(HID, W), v(HID, W), v(4, C, W),
+            v(EXT * C, 2 * W, dtype=bf16), v(6, EXT, C, W), v(2 * W, 6 * W, dtype=bf16), v(C * H, W),
             v(2, 16, 3, 8, W), v(16, 3, 8, W), v(16, 3, 8, W), v(16, 3, 8, W), v(3, 8, W), v(8, 3, 8, W),
             v(TAIL, 8, W), v(16, 2, 8, W), v(8, W), v(8, 8, W), v(EXT, C, W), v(2, C, W), v(C, W),
             DMA(()), DMA(()), DMA((16,)), DMA((16,)), DMA((8,)), DMA((8,)), DMA((16,)), DMA((16,)), DMA(()), DMA(()),
-            DMA((TAIL,)), DMA((16, 2)), DMA((8,)), DMA((8,)), DMA((16, 2)), DMA((TAIL,)),
+            DMA((TAIL,)), DMA((16, 2)), DMA((8,)), DMA((8,)), DMA((16, 2)), DMA((TAIL,)), v(H, C, W), v(21, C, W),
             *buf, *buf,
         ],
         compiler_params=pltpu.CompilerParams(
@@ -907,12 +903,29 @@
     )(*args)
 
 
+PIECES = 4
+
+
 def unpack_kernel(
-    sum_ref, tail_ref, block_hbm, out_hbm, gstem_ref, gstem_b_ref, gdepth_ref, gdepth_b_ref, ggain_ref, gnbias_ref,
-    gexp_ref, gexp_b_ref, gshr_ref, gshr_b_ref, held, sem,
+    sum_hbm, tail_hbm, block_hbm, out_hbm, gstem_ref, gstem_b_ref, gdepth_ref, gdepth_b_ref, ggain_ref, gnbias_ref,
+    gexp_ref, gexp_b_ref, gshr_ref, gshr_b_ref, held, sum_ref, tail_ref, sem,
 ):
-    into = pltpu.make_async_copy(block_hbm, held, sem.at[0])
-    into.start()
+    rows = C * H // PIECES
+
+    def piece(i, back):
+        at = pl.ds(i * rows, rows)
+        if back:
+            return pltpu.make_async_copy(held.at[at], out_hbm.at[at], sem.at[1, i])
+        return pltpu.make_async_copy(block_hbm.at[at], held.at[at], sem.at[0, i])
+
+    total = pltpu.make_async_copy(sum_hbm, sum_ref, sem.at[2, 0])
+    last = pltpu.make_async_copy(tail_hbm, tail_ref, sem.at[2, 1])
+    total.start()
+    last.start()
+    for i in range(PIECES):
+        piece(i, False).start()
+    total.wait()
+    last.wait()
 
     def at(v):
         return sum_ref[v // 48, v % 48 // 3, v % 3]
@@ -922,15 +935,15 @@
         for i in range(12):
             gexp_ref[8 * i : 8 * i + 8, W * j : W * j + W] = at(v)
             v += 1
-        gexp_b_ref[:, W * j : W * j + W] = at(v)[0:1, :]
+        gexp_b_ref[W * j : W * j + W] = at(v)[0]
         v += 1
     for j in range(3):
         for i in range(12):
             gshr_ref[8 * i : 8 * i + 8, W * j : W * j + W] = at(v)
             v += 1
-    into.wait()
-    back = pltpu.make_async_copy(held, out_hbm, sem.at[1])
-    back.start()
+    for i in range(PIECES):
+        piece(i, False).wait()
+        piece(i, True).start()
     for i in range(6):
         gstem_ref[8 * i : 8 * i + 8, :] = tail_ref[i][:, :C]
         gdepth_ref[8 * i : 8 * i + 8, :] = tail_ref[6 + i][:, :C]
@@ -938,19 +951,21 @@
     gdepth_ref[48:49, :] = last[0:1]
     for k, ref in enumerate((gstem_b_ref, gdepth_b_ref, ggain_ref, gnbias_ref, gshr_b_ref)):
         ref[...] = last[k + 1 : k + 2]
-    back.wait()
+    for i in range(PIECES):
+        piece(i, True).wait()
 
 
 def unpack_call(block, total, tail):
     vm = pl.BlockSpec(memory_space=pltpu.VMEM)
     hbm = pl.BlockSpec(memory_space=pltpu.HBM)
-    shapes = ((KK, C), (1, C), (TAPS, C), (1, C), (1, C), (1, C), (C, HID), (1, HID), (C, HID), (1, C))
+    shapes = ((KK, C), (1, C), (TAPS, C), (1, C), (1, C), (1, C), (C, HID), (HID,), (C, HID), (1, C))
     return pl.pallas_call(
         unpack_kernel,
         out_shape=tuple(jax.ShapeDtypeStruct(s, f32) for s in ((C * H, W),) + shapes),
-        in_specs=[vm, vm, hbm],
+        in_specs=[hbm] * 3,
         out_specs=[hbm] + [vm] * len(shapes),
-        scratch_shapes=[pltpu.VMEM((C * H, W), f32), DMA((2,))],
+        scratch_shapes=[
+            pltpu.VMEM((C * H, W), f32), pltpu.VMEM((2, 16, 3, 8, W), f32), pltpu.VMEM((TAIL, 8, W), f32), DMA((3, PIECES))],
         compiler_params=pltpu.CompilerParams(vmem_limit_bytes=56 * 1024 * 1024),
         name="unpack",
     )(total, tail, block)
@@ -966,11 +981,11 @@
 
     block, total, tail = whole_call(
         stored_tiles[0], tile_target, tile_mask, stem_weight, depth_weight, row(stem_bias), row(depth_bias),
-        row(norm_gain), row(norm_bias), expand_weight, row(expand_bias), shrink_weight.T, row(shrink_bias),
+        row(norm_gain), row(norm_bias), expand_weight, expand_bias, shrink_weight.T, row(shrink_bias),
         cotangent.reshape(C * H, W))
     out, gs, gsb, gd, gdb, gg, gn, ge, geb, gh, ghb = unpack_call(block, total, tail)
     return (
-        out.reshape(C, H, W), gs, gsb[0], gd, gdb[0], gg[0], gn[0], ge, geb[0], gh.T, ghb[0],
+        out.reshape(C, H, W), gs, gsb[0], gd, gdb[0], gg[0], gn[0], ge, geb, gh.T, ghb[0],
     )
 
 

time: 82.2 us -> 71.5 us (0.87)
  Pallas kernels: 78.8 us -> 70.7 us
  local copies, waits for them, and re-layouts: 1.91 us -> 0 us
    pallas_call x1, Pallas kernels: 75 us -> 67.9 us  [whole_call(): pl.pallas_call(whole_kernel, out_shape=(s((C * H, W), f32), s((2, 16, 3,...]
    unnamed x4 -> x0, local copies, waits for them, and re-layouts: 1.35 us -> none
    pallas_call x1, Pallas kernels: 3.78 us -> 2.83 us  [unpack_call(): pl.pallas_call(unpack_kernel, out_shape=tuple((jax.ShapeDtypeStruct(s, f3...]
where the time goes in v1:
time: 71.5 us; the launch traced here: 71.3 us
  Pallas kernels  70.7 us (99%)
    pallas_call x1, Pallas kernels, whole_call(): pl.pallas_call(whole_kernel, out_shape=(s((C * H, W), f32), s((2, 16, 3,...  67.9 us
    pallas_call x1, Pallas kernels, unpack_call(): pl.pallas_call(unpack_kernel, out_shape=tuple((jax.ShapeDtypeStruct(s, f3...  2.83 us

profile of v1, /device:TPU:1, one launch (start us, length us, event | category | flops | bytes accessed | tf_op | source)
XLA Modules:
  0.0 71.3 jit_solution(8277265646667299852)
XLA Ops:
  0.6 67.9 %whole.1 = (f32[1536,128]{1,0:T(8,128)}, f32[2,16,3,8,128]{4,3,2,1,0:T(8,128)}, f32[16,8,128]{2,1,0:T(8,128)}) custom-call(f32[8,12288]{1,0:T(8,128)} %bitcast.16, s32[1,8]{1,0:T(1,128)} %target_hbm.1, s32[1,8]{1,0:T(1,128)} %marks_hbm.1, f32[48,96]{1,0:T(8,128)} %stem_hbm.1, f32[49,96]{1,0:T(8,128)} %dw_hbm.1, f32[1,96]{1,0:T(1,128)} %bitcast.18, ...), custom_call_target="tpu_custom_call" | custom-call | tf_op jit(solution)/shard_map/whole/pallas_call | solution.py:878
  68.5 2.8 %unpack.1 = (f32[1536,128]{1,0:T(8,128)}, f32[48,96]{1,0:T(8,128)}, f32[1,96]{1,0:T(1,128)}, f32[49,96]{1,0:T(8,128)}, f32[1,96]{1,0:T(1,128)}, /*index=5*/f32[1...) custom-call(f32[2,16,3,8,128]{4,3,2,1,0:T(8,128)} %get-tuple-element, ...), custom_call_target="tpu_custom_call" | custom-call | tf_op jit(solution)/shard_map/unpack/pallas_call | solution.py:962

commit v2 on v1

--- a/solution.py
+++ b/solution.py
@@ -43,7 +43,7 @@
 
 
 STEM_B, DEPTH_B, GAIN, NBIAS, SHRINK_B = 49, 50, 51, 52, 53
-GROUPS = ((0, 1, 2, 13, 14, 15), (3, 4, 5, 6, 7), (8, 9, 10, 11, 12))
+GROUPS = ((0, 1, 2, 13, 14, 15), (3, 4, 5, 6, 7, 8), (9, 10, 11, 12))
 ORDER = tuple(h for group in GROUPS for h in group)
 INFO = 2
 NEAR = ((0, -1), (0, 1), (-1, -1), (-1, 1), (1, -1), (1, 1))
@@ -104,7 +104,7 @@
     target, marks, stem_v, dw_v, sb_v, db_v, ga_v, nb_v, ew_v, eb_v, sw_v, hb_v, send, recv, edge, edges,
     edges_mid, ct, cot_ref, in_sem, par_sem, tile_send, tile_recv, row_send, row_recv, edge_send, edge_recv,
     mid_send, mid_recv, cot_sem, out_sem, F, FS, D, DSH, DY, GE, GS, ACC, FHL, FSH, SH, OUT, G, R0, B0, R1, B1,
-    R2, TG, TR, TP, TX, DF, DFS, GV, s0, r0, s1, r1, s2, r2, s3, r3, s4, r4, ts1, tr1, ts2, tr2, ts3, tr3, HALO, SPX, *bufs,
+    R2, TG, TR, TP, TX, DF, DFS, GV, s0, r0, s1, r1, s2, r2, s3, r3, s4, r4, ts1, tr1, ts2, tr2, ts3, tr3, SPX, *bufs,
 ):
     gy = lax.axis_index("gy")
     gx = lax.axis_index("gx")
@@ -290,6 +290,42 @@
         pl.semaphore_wait(barrier, greetings)
         for bucket_at in range(2):
             tile_copy(bucket_at, group).start()
+
+    top_ok, bot_ok, ok0, ok1 = validity(gy, gx)
+
+    def stem_of(p, bias):
+        hi, lo = split(p)
+        return dot(stem3_ref[...], jnp.concatenate([hi, lo, hi], axis=0)) + bias
+
+    bias2 = jnp.concatenate([pb_ref[0], pb_ref[0]], axis=1)
+
+    def row_ok(r):
+        return top_ok if r < 3 else bot_ok if r >= H + 3 else None
+
+    def stem_pair(pair):
+        parts = []
+        for q in range(2):
+            ok = row_ok(pair[q])
+            p = pat_ref[pair[q]]
+            parts.append(p if ok is None else jnp.where(ok > 0.0, p, 0.0))
+        y = stem_of(jnp.concatenate(parts, axis=1), bias2)
+        for q in range(2):
+            r = pair[q]
+            ok = row_ok(r)
+            v = y[:, q * W : (q + 1) * W]
+            if ok is not None:
+                v = v * ok
+            F[r] = v
+            hi, lo = split(v)
+            FHL[r * C : (r + 1) * C, 0:W] = hi
+            FHL[r * C : (r + 1) * C, W:] = lo
+    def shift_rows(ref, starts, rows):
+        for n in range(3):
+            for at in starts:
+                y = dot(FHL[at : at + rows, :], SH[:, 2 * n * W : (2 * n + 2) * W])
+                for r in range(rows // C):
+                    ref[2 * n, at // C + r] = y[r * C : (r + 1) * C, :W]
+                    ref[2 * n + 1, at // C + r] = y[r * C : (r + 1) * C, W:]
 
     w16 = lane & 15
     beta = lane >> 4
@@ -370,6 +406,31 @@
         else:
             for i in range(2):
                 mid_copy(group, i).start()
+        for n in range(0, len(rows), 2):
+            stem_pair((rows[n] + 3, rows[n + 1] + 3))
+        for lo, n in row_ranges(group):
+            shift_rows(FSH, ((lo + 3) * C,), n * C)
+
+    def feature_rows(b, which, cs):
+        if b == 3:
+            return {r: F[r, cs, :] for r in which}
+        return {r: FSH[SHIFTS.index(b), r, cs, :] for r in which}
+
+    def conv_block(cb, _):
+        cs = pl.ds(pl.multiple_of(cb * 8, 8), 8)
+        acc = [pb_ref[1, cs, :]] * H
+        for b in range(7):
+            rows = feature_rows(b, range(3, H + 3), cs)
+            for a in range(7):
+                w = wb_ref[7 * a + b, cs, :]
+                for h in range(H):
+                    if h + a in rows:
+                        acc[h] = acc[h] + w * rows[h + a]
+        for h in range(H):
+            D[h, cs, :] = acc[h]
+        return 0
+
+    lax.fori_loop(0, NB, conv_block, 0)
 
     for i in range(len(NEAR)):
         edge_copy(i).wait_recv()
@@ -389,32 +450,8 @@
         side_ref[1, js, :] = jnp.where(prow < 8, roll(mid, -64), roll(bottom, 64))
     row_copy(True).wait_recv()
     row_copy(False).wait_recv()
-    top_ok, bot_ok, ok0, ok1 = validity(gy, gx)
-    def stem_of(p, bias):
-        hi, lo = split(p)
-        return dot(stem3_ref[...], jnp.concatenate([hi, lo, hi], axis=0)) + bias
-
-    bias2 = jnp.concatenate([pb_ref[0], pb_ref[0]], axis=1)
-
-    def row_ok(r):
-        return top_ok if r < 3 else bot_ok if r >= H + 3 else None
-
-    for r in range(0, EXT, 2):
-        parts = []
-        for q in range(2):
-            ok = row_ok(r + q)
-            p = pat_ref[r + q]
-            parts.append(p if ok is None else jnp.where(ok > 0.0, p, 0.0))
-        y = stem_of(jnp.concatenate(parts, axis=1), bias2)
-        for q in range(2):
-            ok = row_ok(r + q)
-            v = y[:, q * W : (q + 1) * W]
-            if ok is not None:
-                v = v * ok
-            F[r + q] = v
-            hi, lo = split(v)
-            FHL[(r + q) * C : (r + q + 1) * C, 0:W] = hi
-            FHL[(r + q) * C : (r + q + 1) * C, W:] = lo
+    for r in (0, 2, 20):
+        stem_pair((r, r + 1) if r != 2 else (2, 19))
     parts = []
     for i, ok in enumerate((ok0, ok1)):
         okk = jnp.concatenate([ok] * (KK // 8), axis=0)
@@ -423,15 +460,8 @@
     for i, ok in enumerate((ok0, ok1)):
         FS[i] = y[:, i * W : (i + 1) * W] * jnp.concatenate([ok] * NB, axis=0)
 
-    def shift_rows(ref, starts, rows):
-        for n in range(3):
-            for at in starts:
-                y = dot(FHL[at : at + rows, :], SH[:, 2 * n * W : (2 * n + 2) * W])
-                for r in range(rows // C):
-                    ref[2 * n, at // C + r] = y[r * C : (r + 1) * C, :W]
-                    ref[2 * n + 1, at // C + r] = y[r * C : (r + 1) * C, W:]
-
-    shift_rows(FSH, (0, 11 * C), 11 * C)
+    for r in (0, H + 3):
+        shift_rows(FSH, (r * C,), 3 * C)
 
     def window(a, lo, hi):
         return jnp.where(prow96 < 11 - a, roll(lo, -8 * a), roll(hi, 8 * (11 - a)))
@@ -454,25 +484,25 @@
                           jnp.where((pos96 >= 3 + k) & (pos96 < 6), roll(part[k], k), 0.0))
     q = jnp.where(left96, roll(q, -3), roll(q, 3))
     for h in range(H):
-        HALO[h] = pb_ref[1] + jnp.where(edge96, roll(q, 125 - 8 * h), 0.0)
-
-    def conv_block(cb, _):
+        D[h] += jnp.where(edge96, roll(q, 125 - 8 * h), 0.0)
+
+    def conv_edge(cb, _):
         cs = pl.ds(pl.multiple_of(cb * 8, 8), 8)
-        acc = [HALO[h, cs, :] for h in range(H)]
+        inner = (0, 1, 2, H - 3, H - 2, H - 1)
+        outer = (0, 1, 2, H + 3, H + 4, H + 5)
+        acc = {h: D[h, cs, :] for h in inner}
         for b in range(7):
-            if b == 3:
-                rows = [F[r, cs, :] for r in range(EXT)]
-            else:
-                rows = [FSH[SHIFTS.index(b), r, cs, :] for r in range(EXT)]
+            rows = feature_rows(b, outer, cs)
             for a in range(7):
                 w = wb_ref[7 * a + b, cs, :]
-                for h in range(H):
-                    acc[h] = acc[h] + w * rows[h + a]
-        for h in range(H):
+                for h in inner:
+                    if h + a in rows:
+                        acc[h] = acc[h] + w * rows[h + a]
+        for h in inner:
             D[h, cs, :] = acc[h]
         return 0
 
-    lax.fori_loop(0, NB, conv_block, 0)
+    lax.fori_loop(0, NB, conv_edge, 0)
 
     fmc = jnp.concatenate([fm_ref[...]] * NB, axis=0)
     ones_row = jnp.where(lax.broadcasted_iota(jnp.int32, (W - C, 2 * W), 0) == 0, 1.0, 0.0)
@@ -894,7 +924,7 @@
             v(2, 16, 3, 8, W), v(16, 3, 8, W), v(16, 3, 8, W), v(16, 3, 8, W), v(3, 8, W), v(8, 3, 8, W),
             v(TAIL, 8, W), v(16, 2, 8, W), v(8, W), v(8, 8, W), v(EXT, C, W), v(2, C, W), v(C, W),
             DMA(()), DMA(()), DMA((16,)), DMA((16,)), DMA((8,)), DMA((8,)), DMA((16,)), DMA((16,)), DMA(()), DMA(()),
-            DMA((TAIL,)), DMA((16, 2)), DMA((8,)), DMA((8,)), DMA((16, 2)), DMA((TAIL,)), v(H, C, W), v(21, C, W),
+            DMA((TAIL,)), DMA((16, 2)), DMA((8,)), DMA((8,)), DMA((16, 2)), DMA((TAIL,)), v(21, C, W),
             *buf, *buf,
         ],
         compiler_params=pltpu.CompilerParams(

time: 71.5 us -> 68 us (0.951)
  Pallas kernels: 70.7 us -> 67.2 us
    pallas_call x1, Pallas kernels: 67.9 us -> 64.3 us  [whole_call(): pl.pallas_call(whole_kernel, out_shape=(s((C * H, W), f32), s((2, 16, 3,...]
where the time goes in v2:
time: 68 us; the launch traced here: 67.8 us
  Pallas kernels  67.2 us (99%)
    pallas_call x1, Pallas kernels, whole_call(): pl.pallas_call(whole_kernel, out_shape=(s((C * H, W), f32), s((2, 16, 3,...  64.3 us
    pallas_call x1, Pallas kernels, unpack_call(): pl.pallas_call(unpack_kernel, out_shape=tuple((jax.ShapeDtypeStruct(s, f3...  2.83 us

profile of v2, /device:TPU:1, one launch (start us, length us, event | category | flops | bytes accessed | tf_op | source)
XLA Modules:
  0.0 67.8 jit_solution(14363297100299717576)
XLA Ops:
  0.6 64.3 %whole.1 = (f32[1536,128]{1,0:T(8,128)}, f32[2,16,3,8,128]{4,3,2,1,0:T(8,128)}, f32[16,8,128]{2,1,0:T(8,128)}) custom-call(f32[8,12288]{1,0:T(8,128)} %bitcast.16, s32[1,8]{1,0:T(1,128)} %target_hbm.1, s32[1,8]{1,0:T(1,128)} %marks_hbm.1, f32[48,96]{1,0:T(8,128)} %stem_hbm.1, f32[49,96]{1,0:T(8,128)} %dw_hbm.1, f32[1,96]{1,0:T(1,128)} %bitcast.18, ...), custom_call_target="tpu_custom_call" | custom-call | tf_op jit(solution)/shard_map/whole/pallas_call | solution.py:908
  65.0 2.8 %unpack.1 = (f32[1536,128]{1,0:T(8,128)}, f32[48,96]{1,0:T(8,128)}, f32[1,96]{1,0:T(1,128)}, f32[49,96]{1,0:T(8,128)}, f32[1,96]{1,0:T(1,128)}, /*index=5*/f32[1...) custom-call(f32[2,16,3,8,128]{4,3,2,1,0:T(8,128)} %get-tuple-element, ...), custom_call_target="tpu_custom_call" | custom-call | tf_op jit(solution)/shard_map/unpack/pallas_call | solution.py:992

commit v3 on v2

--- a/solution.py
+++ b/solution.py
@@ -76,7 +76,7 @@
 XR = W
 CH = 16
 SLOTS = 96
-TAIL = 16
+TAIL = 13
 SHIFTS = (0, 1, 2, 4, 5, 6)
 STEPS = (3,)
 
@@ -286,11 +286,11 @@
             for bucket_at in range(2):
                 tile_copy(bucket_at, group).start()
             continue
-        prepare()
         pl.semaphore_wait(barrier, greetings)
         for bucket_at in range(2):
             tile_copy(bucket_at, group).start()
 
+    prepare()
     top_ok, bot_ok, ok0, ok1 = validity(gy, gx)
 
     def stem_of(p, bias):
@@ -709,29 +709,62 @@
             return [DSH[n, h, cs, :] for h in range(H)]
 
         grads = jnp.zeros((8, W), f32)
-        rows = [F[r, cs, :] for r in range(EXT)]
+        odd = [F[2 * r + 1, cs, :] for r in range(11)]
+        same = [F[2 * r, cs, :] - odd[r] for r in range(11)]
+        next_ = [F[2 * r + 2, cs, :] - odd[r] for r in range(10)]
+
+        def correlate(x, y, j):
+            t = x[0] * y[j]
+            for m in range(1, 8):
+                t = t + x[m] * y[m + j]
+            return t
+
         for b in range(7):
             dd = gradient_rows(b)
-            for a in range(7):
-                if b == 3:
-                    part = None
-                elif b < 3:
-                    part = jnp.where(left, SPX[3 * a + b, cs, :], 0.0)
-                else:
-                    part = jnp.where(left, 0.0, SPX[3 * a + 6 - b, cs, :])
-                for h in range(H):
-                    t = dd[h] * rows[h + a]
-                    part = t if part is None else part + t
-                total = jnp.sum(part, axis=1, keepdims=True)
-                grads = jnp.where(lane == 7 * a + b, total, grads)
-        acc = [DY[r - 3, cs, :] if 3 <= r < H + 3 else None for r in range(EXT)]
+            d0, d1 = dd[0::2], dd[1::2]
+            both = [d0[m] + d1[m] for m in range(8)]
+            for j in range(4):
+                shared = correlate(both, odd, j)
+                for a, part in ((2 * j, (d0, same)), (2 * j + 1, (d1, next_))):
+                    if a == 7:
+                        continue
+                    t = shared + correlate(*part, j)
+                    if b < 3:
+                        t = t + jnp.where(left, SPX[3 * a + b, cs, :], 0.0)
+                    elif b > 3:
+                        t = t + jnp.where(left, 0.0, SPX[3 * a + 6 - b, cs, :])
+                    total = jnp.sum(t, axis=1, keepdims=True)
+                    grads = jnp.where(lane == 7 * a + b, total, grads)
+
+        p0 = [None] * 11
+        p1 = [None] * 10
+        p2 = [None] * 11
+
+        def convolve(p, x, j, w):
+            for m in range(8):
+                t = w * x[m]
+                p[m + j] = t if p[m + j] is None else p[m + j] + t
+
         for b in range(7):
             dd = gradient_rows(b)
-            for a in range(7):
-                w = wb_ref[7 * a + b, cs, :]
-                for h in range(H):
-                    t = w * dd[h]
-                    acc[h + a] = t if acc[h + a] is None else acc[h + a] + t
+            d0, d1 = dd[0::2], dd[1::2]
+            both = [d0[m] + d1[m] for m in range(8)]
+            for j in range(4):
+                w0 = wb_ref[7 * (2 * j) + b, cs, :]
+                convolve(p0, d0, j, w0)
+                if j < 3:
+                    w1 = wb_ref[7 * (2 * j + 1) + b, cs, :]
+                    convolve(p1, d1, j, w1)
+                    w0 = w0 + w1
+                convolve(p2, both, j, w0)
+        acc = []
+        for m in range(11):
+            even = p0[m] if m == 0 else p0[m] + p1[m - 1]
+            other_row = p2[m] - p0[m]
+            if m < 10:
+                other_row = other_row - p1[m]
+            acc += [even, other_row]
+        acc = [t + DY[r - 3, cs, :] if 3 <= r < H + 3 else t for r, t in enumerate(acc)]
         for k, src in enumerate((2, 0, 1, 3)):
             total = jnp.sum(ACC[src, cs, :], axis=1, keepdims=True)
             grads = jnp.where(lane == DEPTH_B + k, total, grads)
@@ -800,13 +833,11 @@
     tail = [gs[8 * i : 8 * i + 8, :] for i in range(6)] + [vec[8 * i : 8 * i + 8, :] for i in range(7)]
     for i, v in enumerate(tail):
         TG[i] = v
-    for i in range(len(tail), TAIL):
-        TG[i] = jnp.zeros((8, W), f32)
 
     def owner(v):
         return at_plane(v, v & 1)
 
-    mine = (plane & 1) == core
+    mine = ((plane & 1) == core) & (plane < TAIL)
 
     def t1(v):
         return rdma(TG.at[v], TR.at[plane, core], ts1.at[v], tr1.at[plane, core], owner(v))

time: 68 us -> 67.7 us (level)
  no operation moved by 1% of the time
where the time goes in v3:
time: 67.7 us; the launch traced here: 67.5 us
  Pallas kernels  66.9 us (99%)
    pallas_call x1, Pallas kernels, whole_call(): pl.pallas_call(whole_kernel, out_shape=(s((C * H, W), f32), s((2, 16, 3,...  64 us
    pallas_call x1, Pallas kernels, unpack_call(): pl.pallas_call(unpack_kernel, out_shape=tuple((jax.ShapeDtypeStruct(s, f3...  2.83 us

profile of v3, /device:TPU:1, one launch (start us, length us, event | category | flops | bytes accessed | tf_op | source)
XLA Modules:
  0.0 67.5 jit_solution(12813253115983334349)
XLA Ops:
  0.6 64.0 %whole.1 = (f32[1536,128]{1,0:T(8,128)}, f32[2,16,3,8,128]{4,3,2,1,0:T(8,128)}, f32[13,8,128]{2,1,0:T(8,128)}) custom-call(f32[8,12288]{1,0:T(8,128)} %bitcast.16, s32[1,8]{1,0:T(1,128)} %target_hbm.1, s32[1,8]{1,0:T(1,128)} %marks_hbm.1, f32[48,96]{1,0:T(8,128)} %stem_hbm.1, f32[49,96]{1,0:T(8,128)} %dw_hbm.1, f32[1,96]{1,0:T(1,128)} %bitcast.18, ...), custom_call_target="tpu_custom_call" | custom-call | tf_op jit(solution)/shard_map/whole/pallas_call | solution.py:939
  64.7 2.8 %unpack.1 = (f32[1536,128]{1,0:T(8,128)}, f32[48,96]{1,0:T(8,128)}, f32[1,96]{1,0:T(1,128)}, f32[49,96]{1,0:T(8,128)}, f32[1,96]{1,0:T(1,128)}, /*index=5*/f32[1...) custom-call(f32[2,16,3,8,128]{4,3,2,1,0:T(8,128)} %get-tuple-element, ...), custom_call_target="tpu_custom_call" | custom-call | tf_op jit(solution)/shard_map/unpack/pallas_call | solution.py:1023

commit v4 on v3

--- a/solution.py
+++ b/solution.py
@@ -78,7 +78,7 @@
 SLOTS = 96
 TAIL = 13
 SHIFTS = (0, 1, 2, 4, 5, 6)
-STEPS = (3,)
+STEPS = (0,)
 
 def validity(gy, gx):
     ny = lax.axis_size("gy")

time: 67.7 us -> 66.6 us (0.984)
  Pallas kernels: 66.9 us -> 65.8 us
    pallas_call x1, Pallas kernels: 64 us -> 63 us  [whole_call(): pl.pallas_call(whole_kernel, out_shape=(s((C * H, W), f32), s((2, 16, 3,...]
where the time goes in v4:
time: 66.6 us; the launch traced here: 66.5 us
  Pallas kernels  65.8 us (99%)
    pallas_call x1, Pallas kernels, whole_call(): pl.pallas_call(whole_kernel, out_shape=(s((C * H, W), f32), s((2, 16, 3,...  63 us
    pallas_call x1, Pallas kernels, unpack_call(): pl.pallas_call(unpack_kernel, out_shape=tuple((jax.ShapeDtypeStruct(s, f3...  2.83 us

profile of v4, /device:TPU:1, one launch (start us, length us, event | category | flops | bytes accessed | tf_op | source)
XLA Modules:
  0.0 66.5 jit_solution(1614296313093153061)
XLA Ops:
  0.6 63.0 %whole.1 = (f32[1536,128]{1,0:T(8,128)}, f32[2,16,3,8,128]{4,3,2,1,0:T(8,128)}, f32[13,8,128]{2,1,0:T(8,128)}) custom-call(f32[8,12288]{1,0:T(8,128)} %bitcast.16, s32[1,8]{1,0:T(1,128)} %target_hbm.1, s32[1,8]{1,0:T(1,128)} %marks_hbm.1, f32[48,96]{1,0:T(8,128)} %stem_hbm.1, f32[49,96]{1,0:T(8,128)} %dw_hbm.1, f32[1,96]{1,0:T(1,128)} %bitcast.18, ...), custom_call_target="tpu_custom_call" | custom-call | tf_op jit(solution)/shard_map/whole/pallas_call | solution.py:939
  63.7 2.8 %unpack.1 = (f32[1536,128]{1,0:T(8,128)}, f32[48,96]{1,0:T(8,128)}, f32[1,96]{1,0:T(1,128)}, f32[49,96]{1,0:T(8,128)}, f32[1,96]{1,0:T(1,128)}, /*index=5*/f32[1...) custom-call(f32[2,16,3,8,128]{4,3,2,1,0:T(8,128)} %get-tuple-element, ...), custom_call_target="tpu_custom_call" | custom-call | tf_op jit(solution)/shard_map/unpack/pallas_call | solution.py:1023
